TPU v7x, 32 devices: a whole 2x2x4 slice. The times are simulated.
32 devices in a mesh: dp: 2 (over y), row: 4 (over x, core), col: 4 (over z).
Axes of the slice: x: 2, y: 2, z: 4, core: 2. Of those that a mesh axis runs over, the one named last changes fastest.
Arguments:
- tokens: bfloat16 [2048, 4096], P(('col', 'row'), 'dp'), may hold values from -6 to 6
- segments: int32 [4096], P('dp'), may hold values from 0 to 12, never falling along the last dimension, each value on 1 to 800 neighbouring positions
- channel_table: bfloat16 [14, 2048], P(None, ('col', 'row')), may hold values from -7.6 to 2
- w_recept: bfloat16 [4, 512, 2048], P(None, 'row', 'col'), may hold values from -0.125 to 0.125
- w_key: bfloat16 [4, 512, 2048], P(None, 'row', 'col'), may hold values from -0.125 to 0.125
- w_value: bfloat16 [4, 512, 2048], P(None, 'row', 'col'), may hold values from -0.125 to 0.125
- w_gate: bfloat16 [4, 512, 2048], P(None, 'row', 'col'), may hold values from -0.125 to 0.125
- w_output: bfloat16 [4, 512, 2048], P(None, 'row', 'col'), may hold values from -0.125 to 0.125
- ffn_key: bfloat16 [4, 1792, 2048], P(None, 'row', 'col'), may hold values from -0.125 to 0.125
- ffn_value: bfloat16 [4, 512, 7168], P(None, 'row', 'col'), may hold values from -0.0625 to 0.0625
- ffn_recept: bfloat16 [4, 512, 2048], P(None, 'row', 'col'), may hold values from -0.125 to 0.125
- cotangent: bfloat16 [2048, 4096], P(('col', 'row'), 'dp'), may hold values from -6 to 6
Outputs:
- mixed: bfloat16 [2048, 4096], P(('col', 'row'), 'dp')
- grad_tokens: float32 [2048, 4096], P(('col', 'row'), 'dp')
- grad_table: float32 [14, 2048], P(None, ('col', 'row'))
- grad_recept: float32 [4, 512, 2048], P(None, 'row', 'col')
- grad_key: float32 [4, 512, 2048], P(None, 'row', 'col')
- grad_value: float32 [4, 512, 2048], P(None, 'row', 'col')
- grad_gate: float32 [4, 512, 2048], P(None, 'row', 'col')
- grad_output: float32 [4, 512, 2048], P(None, 'row', 'col')
- grad_ffn_key: float32 [4, 1792, 2048], P(None, 'row', 'col')
- grad_ffn_value: float32 [4, 512, 7168], P(None, 'row', 'col')
- grad_ffn_recept: float32 [4, 512, 2048], P(None, 'row', 'col')
Inputs may be any that keep to these rules, and one draw needn't show every extreme that they name: `segments`: numbers never fall along the tokens; each document holds 1 to 800 tokens and one holds exactly 800; a document may run past a sequence's end.
All inputs are finite; a program needn't handle non-finite values.
Results may differ from a plain program's by a relative error of at most 0.019.
Values may be sent and summed in bfloat16 or wider, within the bound.
No kernel may reach another device: no remote copies, remote signals or barrier semaphores. Data moves between devices by JAX's collectives and lax.ppermute only.
A program may use at most 192 MiB of HBM per device.

v0:
```python
import jax
import jax.numpy as jnp
from jax import lax
from jax.sharding import PartitionSpec as P

D = 2048
CHANNELS_PER_ATTN = 64
SEQ = 1024
exact_mode = lax.Precision.HIGHEST
norm_eps = 1e-05
group_eps = 0.00064
head_divisor = 8.0
block_len = 64


def feature_sums(stacked):
    return lax.psum(stacked, ("row", "col"))


def norm_forward(payload_entries, gain, bias):
    center = feature_sums(jnp.sum(payload_entries, axis=1)[None])[0] / D
    spread = (
        feature_sums(jnp.sum(jnp.square(payload_entries - center[:, None]), axis=1)[None])[0] / D
    )
    inverse = lax.rsqrt(spread + norm_eps)
    unit_normal = (payload_entries - center[:, None]) * inverse[:, None]
    return (unit_normal * gain + bias, unit_normal, inverse)


def norm_backward(grad_out, unit_normal, inverse, gain):
    grad_unit = grad_out * gain
    totals = feature_sums(
        jnp.stack([jnp.sum(grad_unit, axis=1), jnp.sum(grad_unit * unit_normal, axis=1)])
    )
    grad_in = inverse[:, None] * (
        grad_unit - totals[0][:, None] / D - unit_normal * totals[1][:, None] / D
    )
    return (grad_in, jnp.sum(grad_out * unit_normal, axis=0), jnp.sum(grad_out, axis=0))


def shift_down(payload_entries, handed_onward):
    earlier = jnp.concatenate([jnp.zeros_like(payload_entries[:1]), payload_entries[:-1]], axis=0)
    return earlier * handed_onward[:, None]


def mix_inputs(normed, coeffs, handed_onward):
    shifted = shift_down(normed, handed_onward)
    return normed[None] * coeffs[:, None, :] + shifted[None] * (1.0 - coeffs[:, None, :])


def attention_mixing_segmented(
    ongoing_memory_matrix, segment_portions, logarithmic_fading_speed, extra_current_coeffs
):
    acceptance_entries, lookup_sources, payload_entries, beginning_markers = segment_portions
    positions = jnp.arange(block_len, dtype=jnp.int32)
    start_marks = jnp.where(beginning_markers > 0.5, positions, -1)
    last_start = lax.cummax(start_marks, axis=0)
    steps_in = positions.astype(jnp.float32)[:, None, None]
    scaled_r = acceptance_entries * jnp.exp(logarithmic_fading_speed[None] * steps_in)
    scaled_k = lookup_sources * jnp.exp(-logarithmic_fading_speed[None] * (steps_in + 1.0))
    end_k = lookup_sources * jnp.exp(logarithmic_fading_speed[None] * (block_len - 1.0 - steps_in))
    allowed = (positions[:, None] > positions[None, :]) & (
        last_start[:, None] <= positions[None, :]
    )
    scores = jnp.einsum("thi,shi->hts", scaled_r, scaled_k, precision=exact_mode)
    scores = jnp.where(allowed[None], scores, 0.0)
    intra_term = jnp.einsum("hts,shj->thj", scores, payload_entries, precision=exact_mode)
    diagonal_contribution = (
        jnp.sum(
            acceptance_entries * extra_current_coeffs[None] * lookup_sources, axis=2, keepdims=True
        )
        * payload_entries
    )
    open_start = (last_start < 0).astype(jnp.float32)
    inter_term = (
        jnp.einsum("thi,hij->thj", scaled_r, ongoing_memory_matrix, precision=exact_mode)
        * open_start[:, None, None]
    )
    tail_mask = (positions >= last_start[block_len - 1]).astype(jnp.float32)
    fresh_sum = jnp.einsum(
        "shi,shj->hij", end_k * tail_mask[:, None, None], payload_entries, precision=exact_mode
    )
    carried = (
        ongoing_memory_matrix
        * jnp.exp(logarithmic_fading_speed * block_len)[:, :, None]
        * open_start[block_len - 1]
        + fresh_sum
    )
    return (carried, intra_term + diagonal_contribution + inter_term)


def attention_mixing_complete(
    acceptance_entries,
    lookup_sources,
    payload_entries,
    beginning_markers,
    logarithmic_fading_speed,
    extra_current_coeffs,
):
    block_count = acceptance_entries.shape[0] // block_len

    def reshaped(array_in):
        return array_in.reshape((block_count, block_len) + array_in.shape[1:])

    checked_outcome = jax.checkpoint(attention_mixing_segmented)

    def step_fn(ongoing_memory_matrix, segment_portions):
        return checked_outcome(
            ongoing_memory_matrix, segment_portions, logarithmic_fading_speed, extra_current_coeffs
        )

    initial = jnp.zeros(
        (
            logarithmic_fading_speed.shape[0],
            logarithmic_fading_speed.shape[1],
            logarithmic_fading_speed.shape[1],
        ),
        jnp.float32,
    )
    unused, outputs = lax.scan(
        step_fn,
        initial,
        (
            reshaped(acceptance_entries),
            reshaped(lookup_sources),
            reshaped(payload_entries),
            reshaped(beginning_markers),
        ),
    )
    return outputs.reshape(acceptance_entries.shape)


def time_block(projected, incoming_entries, handed_onward):
    unit_width = projected.shape[1] // 4
    attention_group_total = unit_width // CHANNELS_PER_ATTN
    token_count = projected.shape[0]

    def divide_attention_groups(array_in):
        return array_in.reshape(token_count, attention_group_total, CHANNELS_PER_ATTN)

    acceptance_entries = divide_attention_groups(projected[:, :unit_width])
    lookup_sources = divide_attention_groups(projected[:, unit_width : 2 * unit_width])
    payload_entries = divide_attention_groups(projected[:, 2 * unit_width : 3 * unit_width])
    gate_pre = projected[:, 3 * unit_width :]
    logarithmic_fading_speed = (-jnp.exp(incoming_entries[0])).reshape(
        attention_group_total, CHANNELS_PER_ATTN
    )
    extra_current_coeffs = incoming_entries[1].reshape(attention_group_total, CHANNELS_PER_ATTN)
    combined_attention_groups = (
        attention_mixing_complete(
            acceptance_entries,
            lookup_sources,
            payload_entries,
            1.0 - handed_onward,
            logarithmic_fading_speed,
            extra_current_coeffs,
        )
        / head_divisor
    )
    center = jnp.mean(combined_attention_groups, axis=2, keepdims=True)
    spread = jnp.mean(jnp.square(combined_attention_groups - center), axis=2, keepdims=True)
    grouped = ((combined_attention_groups - center) * lax.rsqrt(spread + group_eps)).reshape(
        token_count, unit_width
    )
    return (grouped * incoming_entries[2] + incoming_entries[3]) * jax.nn.silu(gate_pre)


def project_forward(stack_in, weights):
    gathered = lax.all_gather(stack_in, "row", axis=2, tiled=True)
    partials = [
        jnp.einsum(
            "tk,cwk->tcw", gathered[number], weights[number], preferred_element_type=jnp.float32
        )
        for number in range(len(weights))
    ]
    joined = jnp.concatenate(partials, axis=2)
    summed = lax.psum_scatter(joined, "col", scatter_dimension=1, tiled=True)
    return (gathered, summed[:, 0, :])


def project_backward(grad_out, gathered, weights):
    spread_out = lax.all_gather(grad_out[:, None, :], "col", axis=1, tiled=True)
    offset = 0
    grads_w = []
    grads_in = []
    for number in range(len(weights)):
        columns = weights[number].shape[1]
        block_grad = spread_out[:, :, offset : offset + columns]
        grads_w.append(
            jnp.einsum(
                "tk,tcw->cwk", gathered[number], block_grad, preferred_element_type=jnp.float32
            )
        )
        grads_in.append(
            jnp.einsum(
                "tcw,cwk->tk", block_grad, weights[number], preferred_element_type=jnp.float32
            )
        )
        offset = offset + columns
    summed = lax.psum_scatter(
        jnp.stack(grads_in).astype(jnp.bfloat16), "row", scatter_dimension=2, tiled=True
    ).astype(jnp.float32)
    return (summed, grads_w)


def run_forward(tokens_f, parameter_catalog, weights, handed_onward):
    w_recept, w_key, w_value, w_gate, w_output, ffn_key, ffn_value, ffn_recept = weights
    normed_one, unit_one, inverse_one = norm_forward(
        tokens_f, parameter_catalog[0], parameter_catalog[1]
    )
    mixes_one = mix_inputs(normed_one, parameter_catalog[2:6], handed_onward).astype(jnp.bfloat16)
    gathered_one, projected = project_forward(mixes_one, (w_recept, w_key, w_value, w_gate))
    gated_out = time_block(projected, parameter_catalog[6:10], handed_onward).astype(jnp.bfloat16)
    gathered_gated, branch = project_forward(gated_out[None], (w_output,))
    residual = tokens_f + branch
    normed_two, unit_two, inverse_two = norm_forward(
        residual, parameter_catalog[10], parameter_catalog[11]
    )
    mixes_two = mix_inputs(normed_two, parameter_catalog[12:14], handed_onward).astype(jnp.bfloat16)
    gathered_two, key_recept = project_forward(mixes_two, (ffn_key, ffn_recept))
    hidden_width = ffn_key.shape[1]
    hidden_pre = key_recept[:, :hidden_width]
    recept_pre = key_recept[:, hidden_width:]
    activated = jnp.square(jax.nn.relu(hidden_pre)).astype(jnp.bfloat16)
    gathered_act, payload_mapped = project_forward(activated[None], (ffn_value,))
    output = residual + jax.nn.sigmoid(recept_pre) * payload_mapped
    kept_state = (
        normed_one,
        unit_one,
        inverse_one,
        gathered_one,
        projected,
        gathered_gated,
        normed_two,
        unit_two,
        inverse_two,
        gathered_two,
        hidden_pre,
        recept_pre,
        gathered_act,
        payload_mapped,
    )
    return (output, kept_state)


def shards(
    tokens,
    segments,
    channel_table,
    w_recept,
    w_key,
    w_value,
    w_gate,
    w_output,
    ffn_key,
    ffn_value,
    ffn_recept,
    cotangent,
):
    tokens_f = tokens.astype(jnp.float32).T
    upstream = cotangent.astype(jnp.float32).T
    positions = jnp.arange(tokens_f.shape[0], dtype=jnp.int32)
    earlier = jnp.concatenate([segments[:1], segments[:-1]])
    handed_onward = 1.0 - ((positions % SEQ == 0) | (segments != earlier)).astype(jnp.float32)
    parameter_catalog = channel_table.astype(jnp.float32)
    weights = (w_recept, w_key, w_value, w_gate, w_output, ffn_key, ffn_value, ffn_recept)
    output, unused = run_forward(tokens_f, parameter_catalog, weights, handed_onward)
    tokens_again, upstream, output = lax.optimization_barrier((tokens_f, upstream, output))
    unused_out, kept_state = run_forward(tokens_again, parameter_catalog, weights, handed_onward)
    (
        normed_one,
        unit_one,
        inverse_one,
        gathered_one,
        projected,
        gathered_gated,
        normed_two,
        unit_two,
        inverse_two,
        gathered_two,
        hidden_pre,
        recept_pre,
        gathered_act,
        payload_mapped,
    ) = kept_state
    gate_value = jax.nn.sigmoid(recept_pre)
    grad_valued = (upstream * gate_value).astype(jnp.bfloat16)
    grad_recept = upstream * payload_mapped * gate_value * (1.0 - gate_value)
    grad_act, grads_value = project_backward(grad_valued, gathered_act, (ffn_value,))
    grad_hidden = grad_act[0] * 2.0 * jax.nn.relu(hidden_pre)
    grad_key_recept = jnp.concatenate([grad_hidden, grad_recept], axis=1).astype(jnp.bfloat16)
    grad_mixes_two, grads_ffn = project_backward(
        grad_key_recept, gathered_two, (ffn_key, ffn_recept)
    )
    unused_two, second_pull = jax.vjp(
        lambda normed, coeffs: mix_inputs(normed, coeffs, handed_onward),
        normed_two,
        parameter_catalog[12:14],
    )
    grad_normed_two, grad_coeff_two = second_pull(grad_mixes_two)
    grad_res_norm, gain_two, bias_two = norm_backward(
        grad_normed_two, unit_two, inverse_two, parameter_catalog[10]
    )
    grad_residual = upstream + grad_res_norm
    grad_gated, grads_output = project_backward(
        grad_residual.astype(jnp.bfloat16), gathered_gated, (w_output,)
    )
    unused_block, block_pull = jax.vjp(
        lambda projected_in, incoming_entries: time_block(
            projected_in, incoming_entries, handed_onward
        ),
        projected,
        parameter_catalog[6:10],
    )
    grad_projected, grad_rows = block_pull(grad_gated[0])
    grad_mixes_one, grads_time = project_backward(
        grad_projected.astype(jnp.bfloat16), gathered_one, (w_recept, w_key, w_value, w_gate)
    )
    unused_one, first_pull = jax.vjp(
        lambda normed, coeffs: mix_inputs(normed, coeffs, handed_onward),
        normed_one,
        parameter_catalog[2:6],
    )
    grad_normed_one, grad_coeff_one = first_pull(grad_mixes_one)
    grad_tok_norm, gain_one, bias_one = norm_backward(
        grad_normed_one, unit_one, inverse_one, parameter_catalog[0]
    )
    grad_tokens = grad_residual + grad_tok_norm
    table_grad = jnp.concatenate(
        [
            gain_one[None],
            bias_one[None],
            grad_coeff_one,
            grad_rows,
            gain_two[None],
            bias_two[None],
            grad_coeff_two,
        ],
        axis=0,
    )
    summed = (
        lax.psum(grads_time[0].astype(jnp.bfloat16), "dp").astype(jnp.float32),
        lax.psum(grads_time[1].astype(jnp.bfloat16), "dp").astype(jnp.float32),
        lax.psum(grads_time[2].astype(jnp.bfloat16), "dp").astype(jnp.float32),
        lax.psum(grads_time[3].astype(jnp.bfloat16), "dp").astype(jnp.float32),
        lax.psum(grads_output[0].astype(jnp.bfloat16), "dp").astype(jnp.float32),
        lax.psum(grads_ffn[0].astype(jnp.bfloat16), "dp").astype(jnp.float32),
        lax.psum(grads_value[0].astype(jnp.bfloat16), "dp").astype(jnp.float32),
        lax.psum(grads_ffn[1].astype(jnp.bfloat16), "dp").astype(jnp.float32),
        lax.psum(table_grad.astype(jnp.bfloat16), "dp").astype(jnp.float32),
    )
    return (
        output.astype(jnp.bfloat16).T,
        grad_tokens.T,
        summed[8],
        summed[0],
        summed[1],
        summed[2],
        summed[3],
        summed[4],
        summed[5],
        summed[6],
        summed[7],
    )


def solution(mesh):
    in_specs = (
        P(("col", "row"), "dp"),
        P("dp"),
        P(None, ("col", "row")),
        P(None, "row", "col"),
        P(None, "row", "col"),
        P(None, "row", "col"),
        P(None, "row", "col"),
        P(None, "row", "col"),
        P(None, "row", "col"),
        P(None, "row", "col"),
        P(None, "row", "col"),
        P(("col", "row"), "dp"),
    )
    out_specs = (
        P(("col", "row"), "dp"),
        P(("col", "row"), "dp"),
        P(None, ("col", "row")),
        P(None, "row", "col"),
        P(None, "row", "col"),
        P(None, "row", "col"),
        P(None, "row", "col"),
        P(None, "row", "col"),
        P(None, "row", "col"),
        P(None, "row", "col"),
        P(None, "row", "col"),
    )
    return jax.shard_map(shards, mesh=mesh, in_specs=in_specs, out_specs=out_specs, check_vma=False)
```

profile of v0, /device:TPU:0, one launch (start us, length us, event | category | flops | bytes accessed | tf_op | source)
XLA Modules:
  0.0 4988.6 jit_solution(13791718364554033619)
XLA Ops:
  12.2 36.0 psum.133
  90.2 58.4 %all-gather.20.cloned.1.call-done = bf16[4,2048,512]{2,1,0:T(8,128)(2,1)} async-done(((bf16[4,2048,128]{2,1,0:T(8,128)(2,1)}), bf16[4,2048,512]{2,1,0:T(8,128)(2,1)}) %all-gather.20.cloned.1.call-update) | async-done | bytes 8388624 | tf_op jit(solution)/shard_map/all_gather | solution.py:169
  165.3 278.8 %reduce-scatter.17.cloned.1.call-done = f32[2048,1,512]{0,2,1:T(8,128)} async-done(((f32[2048,4,512]{0,2,1:T(8,128)}), f32[2048,1,512]{0,2,1:T(8,128)}) %reduce-scatter.17.cloned.1.call-update) | async-done | bytes 4194320 | tf_op jit(solution)/shard_map/reduce_scatter | solution.py:177
  457.3 281.5 %while.72 = (s32[]{:T(128)}, f32[2,64,64]{2,1,0:T(8,128)S(1)}, f32[32,64,2,64]{3,1,2,0:T(8,128)}, f32[2,64]{1,0:T(2,128)S(1)}, f32[32,64]{1,0:T(8,128)S(1)}, /*i...) while((s32[]{:T(128)}, f32[2,64,64]{2,1,0:T(8,128)S(1)}, ...), condition=%wide.region_8.9_spmd.clone, body=%wide.region_5.8_spmd.clone.sunk | while | flops 25355200 | bytes 1069532 | solution.py:120
  782.2 76.1 %reduce-scatter.19.cloned.1.call-done = f32[2048,1,128]{0,2,1:T(8,128)} async-done(((f32[2048,4,128]{0,2,1:T(8,128)}), f32[2048,1,128]{0,2,1:T(8,128)}) %reduce-scatter.19.cloned.1.call-update) | async-done | bytes 1048592 | tf_op jit(solution)/shard_map/reduce_scatter | solution.py:177
  859.8 33.6 psum.135
  934.9 33.7 all-gather.22.cloned.1.call-done
  983.0 313.9 %reduce-scatter.21.cloned.1.call-done = f32[2048,1,576]{0,2,1:T(8,128)} async-done(((f32[2048,4,576]{0,2,1:T(8,128)}), f32[2048,1,576]{0,2,1:T(8,128)}) %reduce-scatter.21.cloned.1.call-update) | async-done | bytes 4718608 | tf_op jit(solution)/shard_map/reduce_scatter | solution.py:177
  1300.7 53.5 %all-gather.32.cloned.1.call-done = bf16[2048,1792]{0,1:T(8,128)(2,1)} async-done(((bf16[2048,448]{0,1:T(8,128)(2,1)}), bf16[2048,1792]{0,1:T(8,128)(2,1)}) %all-gather.32.cloned.1.call-update) | async-done | bytes 7340048 | tf_op jit(solution)/shard_map/all_gather | solution.py:169
  1366.5 74.2 %reduce-scatter.23.cloned.1.call-done = f32[2048,1,128]{0,2,1:T(8,128)} async-done(((f32[2048,4,128]{0,2,1:T(8,128)}), f32[2048,1,128]{0,2,1:T(8,128)}) %reduce-scatter.23.cloned.1.call-update) | async-done | bytes 1048592 | tf_op jit(solution)/shard_map/reduce_scatter | solution.py:177
  1443.8 33.6 psum.137
  1520.4 58.6 %all-gather.24.cloned.1.call-done = bf16[4,2048,512]{2,1,0:T(8,128)(2,1)} async-done(((bf16[4,2048,128]{2,1,0:T(8,128)(2,1)}), bf16[4,2048,512]{2,1,0:T(8,128)(2,1)}) %all-gather.24.cloned.1.call-update) | async-done | bytes 8388624 | tf_op jit(solution)/shard_map/all_gather | solution.py:169
  1594.7 279.7 %reduce-scatter.25.cloned.1.call-done = f32[2048,1,512]{0,2,1:T(8,128)} async-done(((f32[2048,4,512]{0,2,1:T(8,128)}), f32[2048,1,512]{0,2,1:T(8,128)}) %reduce-scatter.25.cloned.1.call-update) | async-done | bytes 4194320 | tf_op jit(solution)/shard_map/reduce_scatter | solution.py:177
  1898.1 355.7 %while.73 = (s32[]{:T(128)}, f32[2,64,64]{2,1,0:T(8,128)S(1)}, f32[32,64,2,64]{3,1,2,0:T(8,128)}, f32[2,64]{1,0:T(2,128)S(1)}, f32[32,64]{1,0:T(8,128)}, /*index...) while((s32[]{:T(128)}, f32[2,64,64]{2,1,0:T(8,128)S(1)}, ...), condition=%wide.region_26.27_spmd.clone, body=%wide.region_23.26_spmd.clone.sunk | while | flops 25355200 | bytes 975315 | solution.py:120
  2255.4 331.4 %while.75 = (s32[]{:T(128)}, f32[2,64,64]{2,1,0:T(8,128)S(1)}, f32[32,64,2,64]{3,1,2,0:T(8,128)}, f32[32,2,64,64]{3,2,1,0:T(8,128)}, f32[2,64,1]{1,0,2:T(2,128)S...) while((s32[]{:T(128)}, f32[2,64,64]{2,1,0:T(8,128)S(1)}, ...), condition=%wide.region_46.47_spmd.clone.clone.clone.clone, body=%wide.region_43.46_spmd.clone.clone.clone.clone.sunk | while | flops 25362944 | bytes 1068772 | solution.py:120
  2631.7 76.9 %reduce-scatter.27.cloned.1.call-done = f32[2048,1,128]{0,2,1:T(8,128)} async-done(((f32[2048,4,128]{0,2,1:T(8,128)}), f32[2048,1,128]{0,2,1:T(8,128)}) %reduce-scatter.27.cloned.1.call-update) | async-done | bytes 1048592 | tf_op jit(solution)/shard_map/reduce_scatter | solution.py:177
  2710.9 34.0 psum.139
  2786.1 34.1 all-gather.26.cloned.1.call-done
  2834.6 313.9 %reduce-scatter.29.cloned.1.call-done = f32[2048,1,576]{0,2,1:T(8,128)} async-done(((f32[2048,4,576]{0,2,1:T(8,128)}), f32[2048,1,576]{0,2,1:T(8,128)}) %reduce-scatter.29.cloned.1.call-update) | async-done | bytes 4718608 | tf_op jit(solution)/shard_map/reduce_scatter | solution.py:177
  3152.2 53.5 %all-gather.38.cloned.1.call-done = bf16[2048,1792]{0,1:T(8,128)(2,1)} async-done(((bf16[2048,448]{0,1:T(8,128)(2,1)}), bf16[2048,1792]{0,1:T(8,128)(2,1)}) %all-gather.38.cloned.1.call-update) | async-done | bytes 7340048 | tf_op jit(solution)/shard_map/all_gather | solution.py:169
  3215.3 76.9 %reduce-scatter.33.cloned.1.call-done = f32[2048,1,128]{0,2,1:T(8,128)} async-done(((f32[2048,4,128]{0,2,1:T(8,128)}), f32[2048,1,128]{0,2,1:T(8,128)}) %reduce-scatter.33.cloned.1.call-update) | async-done | bytes 1048592 | tf_op jit(solution)/shard_map/reduce_scatter | solution.py:177
  3295.2 46.4 all-gather.36.cloned.1.call-done
  3350.8 64.3 %reduce-scatter.31.cloned.1.call-done = bf16[1,2048,448]{1,2,0:T(8,128)(2,1)} async-done(((bf16[1,2048,1792]{1,2,0:T(8,128)(2,1)}), bf16[1,2048,448]{1,2,0:T(8,128)(2,1)}) %reduce-scatter.31.cloned.1.call-update) | async-done | bytes 1835024 | tf_op jit(solution)/shard_map/reduce_scatter | solution.py:200
  3420.1 166.9 %all-gather.28.cloned.1.call-done = bf16[2048,4,576]{0,2,1:T(8,128)(2,1)} async-done(((bf16[2048,1,576]{0,2,1:T(8,128)(2,1)}), bf16[2048,4,576]{0,2,1:T(8,128)(2,1)}) %all-gather.28.cloned.1.call-update) | async-done | bytes 9437200 | tf_op jit(solution)/shard_map/all_gather | solution.py:182
  3616.1 42.7 reduce-scatter.37.cloned.1.call-done
  3678.0 60.7 %psum.141 = f32[2,2048]{1,0:T(2,128)S(1)} all-reduce(f32[2,2048]{1,0:T(2,128)S(1)} %pad_maximum_fusion.7), channel_id=1, replica_groups=mesh['dp'=2,'row'=4,'col'=4] {'row','col'}, use_global_device_ids=true, to_apply=%region_42.43 | all-reduce | flops 4096 | bytes 32768 | tf_op jit(solution)/shard_map/psum | solution.py:17
  3741.5 44.3 all-gather.40.cloned.1.call-done
  3842.9 629.8 %while.74 = (s32[]{:T(128)}, f32[2,64]{1,0:T(2,128)S(1)}, f32[2,64]{1,0:T(2,128)S(1)}, f32[2,64,64]{2,1,0:T(8,128)S(1)}, f32[32,64,2,64]{1,0,3,2:T(8,128)}, /*in...) while((s32[]{:T(128)}, f32[2,64]{1,0:T(2,128)S(1)}, ...), condition=%wide.region_62.63_spmd.clone, body=%wide.region_53.62_spmd.clone.sunk | while | flops 57132356 | bytes 2100241 | solution.py:120
  4508.6 126.1 %all-gather.42.cloned.1.call-done = bf16[2048,2048]{0,1:T(8,128)(2,1)} async-done(((bf16[2048,512]{0,1:T(8,128)(2,1)}), bf16[2048,2048]{0,1:T(8,128)(2,1)}) %all-gather.42.cloned.1.call-update) | async-done | bytes 8388624 | tf_op jit(solution)/shard_map/all_gather | solution.py:182
  4697.2 119.0 %all-reduce.17.cloned.1.call-done = (bf16[4,128,512]{2,1,0:T(8,128)(2,1)}, bf16[4,128,512]{2,1,0:T(8,128)(2,1)}, bf16[4,128,512]{2,1,0:T(8,128)(2,1)}, bf16[4,12...) async-done(((bf16[4,128,512]{2,1,0:T(8,128)(2,1)}, ...) | async-done | bytes 6815760 | tf_op jit(solution)/shard_map/psum | solution.py:342
  4829.9 60.6 %reduce-scatter.39.cloned.1.call-done = bf16[128,8192]{1,0:T(8,128)(2,1)} async-done(((bf16[512,8192]{1,0:T(8,128)(2,1)}), bf16[128,8192]{1,0:T(8,128)(2,1)}) %reduce-scatter.39.cloned.1.call-update) | async-done | bytes 2097168
  4912.4 60.7 %psum.142 = f32[2,2048]{1,0:T(2,128)S(1)} all-reduce(f32[2,2048]{1,0:T(2,128)S(1)} %pad_maximum_fusion.8), channel_id=1, replica_groups=mesh['dp'=2,'row'=4,'col'=4] {'row','col'}, use_global_device_ids=true, to_apply=%region_68.69 | all-reduce | flops 4096 | bytes 32768 | tf_op jit(solution)/shard_map/psum | solution.py:17
  (3664 shorter events, 2249.7 us)
Async XLA Ops:
  7.2 964.5 %copy-start = (bf16[4,448,512]{2,1,0:T(8,128)(2,1)S(1)}, bf16[4,448,512]{2,1,0:T(8,128)(2,1)}, u32[]{:S(2)}) copy-start(bf16[4,448,512]{2,1,0:T(8,128)(2,1)} %param.28) | copy-start | bytes 5505028
  7.2 141.4 %all-gather.20.cloned.1.call-start = ((), (), s32[]{:S(2)}) async-start(), calls=%async_computation.12 | async-start | bytes 10485760 | tf_op jit(solution)/shard_map/all_gather | solution.py:169
  8.1 774.2 %copy-start.41 = (f32[14,128]{1,0:T(8,128)}, f32[14,128]{1,0:T(8,128)S(1)}, u32[]{:S(2)}) copy-start(f32[14,128]{1,0:T(8,128)S(1)} %convert_element_type.306) | copy-start | bytes 21508
  9.1 915.0 %copy-start.45 = (f32[128]{0:T(128)}, f32[128]{0:T(128)S(1)}, u32[]{:S(2)}) copy-start(f32[128]{0:T(128)S(1)} %get-tuple-element.1371) | copy-start | bytes 1540
  9.1 1499.0 %copy-start.43 = (f32[128]{0:T(128)}, f32[128]{0:T(128)S(1)}, u32[]{:S(2)}) copy-start(f32[128]{0:T(128)S(1)} %get-tuple-element.1369) | copy-start | bytes 1540
  9.1 1507.8 %copy-start.36 = (f32[4,128]{1,0:T(4,128)}, f32[4,128]{1,0:T(4,128)S(1)}, u32[]{:S(2)}) copy-start(f32[4,128]{1,0:T(4,128)S(1)} %broadcast_subtract_fusion.4) | copy-start | bytes 6148
  9.8 1507.1 %copy-start.38 = (f32[4,128]{1,0:T(4,128)}, f32[4,128]{1,0:T(4,128)S(1)}, u32[]{:S(2)}) copy-start(f32[4,128]{1,0:T(4,128)S(1)} %slice.306) | copy-start | bytes 6148
  90.2 353.9 %reduce-scatter.17.cloned.1.call-start = ((), (), s32[]{:S(2)}) async-start(), calls=%async_computation.13 | async-start | bytes 20971520 | tf_op jit(solution)/shard_map/reduce_scatter | solution.py:177
  163.7 613.0 %all-gather.30.cloned.1.call-start = ((), (), s32[]{:S(2)}) async-start(), calls=%async_computation.27 | async-start | bytes 2621440 | tf_op jit(solution)/shard_map/all_gather | solution.py:169
  753.2 105.2 %reduce-scatter.19.cloned.1.call-start = ((), (), s32[]{:S(2)}) async-start(), calls=%async_computation.14 | async-start | bytes 5242880 | tf_op jit(solution)/shard_map/reduce_scatter | solution.py:177
  781.4 187.2 %all-gather.22.cloned.1.call-start = ((), (), s32[]{:S(2)}) async-start(), calls=%async_computation.15 | async-start | bytes 5242880 | tf_op jit(solution)/shard_map/all_gather | solution.py:169
  934.4 362.5 %reduce-scatter.21.cloned.1.call-start = ((), (), s32[]{:S(2)}) async-start(), calls=%async_computation.16 | async-start | bytes 23592960 | tf_op jit(solution)/shard_map/reduce_scatter | solution.py:177
  983.0 371.2 %all-gather.32.cloned.1.call-start = ((), (), s32[]{:S(2)}) async-start(), calls=%async_computation.28 | async-start | bytes 9175040 | tf_op jit(solution)/shard_map/all_gather | solution.py:169
  1300.6 140.1 %reduce-scatter.23.cloned.1.call-start = ((), (), s32[]{:S(2)}) async-start(), calls=%async_computation.17 | async-start | bytes 5242880 | tf_op jit(solution)/shard_map/reduce_scatter | solution.py:177
  1363.9 215.1 %all-gather.24.cloned.1.call-start = ((), (), s32[]{:S(2)}) async-start(), calls=%async_computation.18 | async-start | bytes 10485760 | tf_op jit(solution)/shard_map/all_gather | solution.py:169
  1364.0 1344.5 %copy-start.2 = (f32[2048,128]{0,1:T(8,128)}, f32[2048,128]{0,1:T(8,128)S(1)}, u32[]{:S(2)}) copy-start(f32[2048,128]{0,1:T(8,128)S(1)} %convert_bitcast_fusion) | copy-start | bytes 3145732
  1520.4 354.1 %reduce-scatter.25.cloned.1.call-start = ((), (), s32[]{:S(2)}) async-start(), calls=%async_computation.19 | async-start | bytes 20971520 | tf_op jit(solution)/shard_map/reduce_scatter | solution.py:177
  1594.0 1032.7 %all-gather.34.cloned.1.call-start = ((), (), s32[]{:S(2)}) async-start(), calls=%async_computation.29 | async-start | bytes 2621440 | tf_op jit(solution)/shard_map/all_gather | solution.py:169
  2603.2 105.3 %reduce-scatter.27.cloned.1.call-start = ((), (), s32[]{:S(2)}) async-start(), calls=%async_computation.20 | async-start | bytes 5242880 | tf_op jit(solution)/shard_map/reduce_scatter | solution.py:177
  2631.7 188.6 %all-gather.26.cloned.1.call-start = ((), (), s32[]{:S(2)}) async-start(), calls=%async_computation.21 | async-start | bytes 5242880 | tf_op jit(solution)/shard_map/all_gather | solution.py:169
  2786.1 362.4 %reduce-scatter.29.cloned.1.call-start = ((), (), s32[]{:S(2)}) async-start(), calls=%async_computation.22 | async-start | bytes 23592960 | tf_op jit(solution)/shard_map/reduce_scatter | solution.py:177
  2834.5 371.2 %all-gather.38.cloned.1.call-start = ((), (), s32[]{:S(2)}) async-start(), calls=%async_computation.31 | async-start | bytes 9175040 | tf_op jit(solution)/shard_map/all_gather | solution.py:169
  3152.2 140.0 %reduce-scatter.33.cloned.1.call-start = ((), (), s32[]{:S(2)}) async-start(), calls=%async_computation.24 | async-start | bytes 5242880 | tf_op jit(solution)/shard_map/reduce_scatter | solution.py:177
  3215.3 126.3 %all-gather.36.cloned.1.call-start = ((), (), s32[]{:S(2)}) async-start(), calls=%async_computation.30 | async-start | bytes 2621440 | tf_op jit(solution)/shard_map/all_gather | solution.py:182
  3295.0 120.1 %reduce-scatter.31.cloned.1.call-start = ((), (), s32[]{:S(2)}) async-start(), calls=%async_computation.23 | async-start | bytes 9175040 | tf_op jit(solution)/shard_map/reduce_scatter | solution.py:200
  3350.7 236.3 %all-gather.28.cloned.1.call-start = ((), (), s32[]{:S(2)}) async-start(), calls=%async_computation.25 | async-start | bytes 11796480 | tf_op jit(solution)/shard_map/all_gather | solution.py:182
  3420.0 238.7 %reduce-scatter.37.cloned.1.call-start = ((), (), s32[]{:S(2)}) async-start(), calls=%async_computation.34 | async-start | bytes 5242880
  3615.9 169.9 %all-gather.40.cloned.1.call-start = ((), (), s32[]{:S(2)}) async-start(), calls=%async_computation.32 | async-start | bytes 2621440 | tf_op jit(solution)/shard_map/all_gather | solution.py:182
  3741.5 78.9 %reduce-scatter.35.cloned.1.call-start = ((), (), s32[]{:S(2)}) async-start(), calls=%async_computation.26 | async-start | bytes 2621440 | tf_op jit(solution)/shard_map/reduce_scatter | solution.py:200
  3790.1 844.6 %all-gather.42.cloned.1.call-start = ((), (), s32[]{:S(2)}) async-start(), calls=%async_computation.33 | async-start | bytes 10485760 | tf_op jit(solution)/shard_map/all_gather | solution.py:182
  4484.9 331.3 %all-reduce.17.cloned.1.call-start = ((), (), s32[]{:S(2)}) async-start(), calls=%async_computation.36 | async-start | bytes 13631488 | tf_op jit(solution)/shard_map/psum | solution.py:342
  4650.9 239.7 %reduce-scatter.39.cloned.1.call-start = ((), (), s32[]{:S(2)}) async-start(), calls=%async_computation.35 | async-start | bytes 10485760
  (71 other events, 1018.4 us)
Sparse Core Ops, SparseCore 0:
  90.3 58.2 all-gather.19
  163.8 280.2 reduce-scatter.16
  753.3 23.2 all-gather.29
  781.6 76.7 reduce-scatter.18
  934.5 33.9 all-gather.21
  983.1 313.7 reduce-scatter.20
  1300.8 53.3 all-gather.31
  1364.0 76.7 reduce-scatter.22
  1520.5 58.4 all-gather.23
  1594.1 280.2 reduce-scatter.24
  2603.3 23.3 all-gather.33
  2631.8 76.7 reduce-scatter.26
  2786.2 33.9 all-gather.25
  2834.6 313.7 reduce-scatter.28
  3152.3 53.3 all-gather.37
  3215.4 76.7 reduce-scatter.32
  3295.1 46.4 all-gather.35
  3350.8 64.1 reduce-scatter.30
  3420.2 166.7 all-gather.27
  3616.1 42.6 reduce-scatter.36
  3741.6 44.1 all-gather.39
  3790.2 30.1 reduce-scatter.34
  4485.0 149.6 all-gather.41
  4651.0 165.1 all-reduce.16
  4818.8 71.7 reduce-scatter.38
where the time goes:
time: 5030 us; the launch traced here: 4990 us
  waiting for transfers between devices  2520 us (50%)
  local copies, waits for them, and re-layouts  886 us (18%)
  matrix products  629 us (13%)
  other arithmetic  539 us (11%)
  blocking collectives  385 us (8%)
    reduce_scatter x8, waiting for transfers between devices, project_forward(): summed = lax.psum_scatter(joined, 'col', scatter_dimension=1, tiled=True)  1490 us
    all_gather x4, waiting for transfers between devices, project_backward(): spread_out = lax.all_gather(grad_out[:, None, :], 'col', axis=1, tiled=True)  384 us
    psum x10, blocking collectives, feature_sums(): return lax.psum(stacked, ('row', 'col'))  380 us
    all_gather x8, waiting for transfers between devices, project_forward(): gathered = lax.all_gather(stack_in, 'row', axis=2, tiled=True)  339 us
    dynamic_update_slice x160, local copies, waits for them, and re-layouts, attention_mixing_complete(): lax.scan(step_fn, initial, (reshaped(acceptance_entries), reshaped(lookup...  282 us
    dot_general x160, matrix products, attention_mixing_segmented(): jnp.einsum('shi,shj->hij', end_k * tail_mask[:, None, None], payload_entr...  173 us
    dynamic_slice x256, local copies, waits for them, and re-layouts, attention_mixing_complete(): lax.scan(step_fn, initial, (reshaped(acceptance_entries), reshaped(lookup...  149 us
    mul x96, other arithmetic, attention_mixing_segmented(): jnp.sum(acceptance_entries * extra_current_coeffs[None] * lookup_sources,...  127 us
  transfers between devices with their start and end apart: 25, of which 25 were waited for; matrix products, arithmetic and copies ran while one was open for 2% of the time, Pallas kernels for 0%

commit v1 on v0

--- a/solution.py
+++ b/solution.py
@@ -14,7 +14,7 @@
 
 
 def feature_sums(stacked):
-    return lax.psum(stacked, ("row", "col"))
+    return jnp.sum(lax.all_gather(stacked, ("row", "col")), axis=0)
 
 
 def norm_forward(payload_entries, gain, bias):

time: 5030 us -> 4970 us (0.988)
  blocking collectives: 385 us -> 324 us
    psum x10 -> x0, blocking collectives: 380 us -> none  [feature_sums(): return lax.psum(stacked, ('row', 'col'))]
    all_gather x0 -> x10, blocking collectives: none -> 319 us  [feature_sums(): return jnp.sum(lax.all_gather(stacked, ('row', 'col')), axis=0)]
where the time goes in v1:
time: 4970 us; the launch traced here: 4930 us
  waiting for transfers between devices  2520 us (51%)
  local copies, waits for them, and re-layouts  891 us (18%)
  matrix products  629 us (13%)
  other arithmetic  543 us (11%)
  blocking collectives  324 us (7%)
    reduce_scatter x8, waiting for transfers between devices, project_forward(): summed = lax.psum_scatter(joined, 'col', scatter_dimension=1, tiled=True)  1490 us
    all_gather x4, waiting for transfers between devices, project_backward(): spread_out = lax.all_gather(grad_out[:, None, :], 'col', axis=1, tiled=True)  383 us
    all_gather x8, waiting for transfers between devices, project_forward(): gathered = lax.all_gather(stack_in, 'row', axis=2, tiled=True)  339 us
    all_gather x10, blocking collectives, feature_sums(): return jnp.sum(lax.all_gather(stacked, ('row', 'col')), axis=0)  319 us
    dynamic_update_slice x160, local copies, waits for them, and re-layouts, attention_mixing_complete(): lax.scan(step_fn, initial, (reshaped(acceptance_entries), reshaped(lookup...  282 us
    dot_general x160, matrix products, attention_mixing_segmented(): jnp.einsum('shi,shj->hij', end_k * tail_mask[:, None, None], payload_entr...  173 us
    dynamic_slice x256, local copies, waits for them, and re-layouts, attention_mixing_complete(): lax.scan(step_fn, initial, (reshaped(acceptance_entries), reshaped(lookup...  149 us
    mul x96, other arithmetic, attention_mixing_segmented(): jnp.sum(acceptance_entries * extra_current_coeffs[None] * lookup_sources,...  127 us
  transfers between devices with their start and end apart: 25, of which 25 were waited for; matrix products, arithmetic and copies ran while one was open for 2% of the time, Pallas kernels for 0%

profile of v1, /device:TPU:0, one launch (start us, length us, event | category | flops | bytes accessed | tf_op | source)
XLA Modules:
  0.0 4934.7 jit_solution(14432998060767174255)
XLA Ops:
  12.2 35.0 all-gather
  87.6 58.3 %all-gather.32.cloned.1.call-done = bf16[4,2048,512]{2,1,0:T(8,128)(2,1)} async-done(((bf16[4,2048,128]{2,1,0:T(8,128)(2,1)}), bf16[4,2048,512]{2,1,0:T(8,128)(2,1)}) %all-gather.32.cloned.1.call-update) | async-done | bytes 8388624 | tf_op jit(solution)/shard_map/all_gather | solution.py:169
  162.0 279.3 %reduce-scatter.17.cloned.1.call-done = f32[2048,1,512]{0,2,1:T(8,128)} async-done(((f32[2048,4,512]{0,2,1:T(8,128)}), f32[2048,1,512]{0,2,1:T(8,128)}) %reduce-scatter.17.cloned.1.call-update) | async-done | bytes 4194320 | tf_op jit(solution)/shard_map/reduce_scatter | solution.py:177
  455.5 281.5 %while.72 = (s32[]{:T(128)}, f32[2,64,64]{2,1,0:T(8,128)S(1)}, f32[32,64,2,64]{3,1,2,0:T(8,128)}, f32[2,64]{1,0:T(2,128)S(1)}, f32[32,64]{1,0:T(8,128)S(1)}, /*i...) while((s32[]{:T(128)}, f32[2,64,64]{2,1,0:T(8,128)S(1)}, ...), condition=%wide.region_8.9_spmd.clone, body=%wide.region_5.8_spmd.clone.sunk | while | flops 25355200 | bytes 1069532 | solution.py:120
  782.5 75.1 %reduce-scatter.19.cloned.1.call-done = f32[2048,1,128]{0,2,1:T(8,128)} async-done(((f32[2048,4,128]{0,2,1:T(8,128)}), f32[2048,1,128]{0,2,1:T(8,128)}) %reduce-scatter.19.cloned.1.call-update) | async-done | bytes 1048592 | tf_op jit(solution)/shard_map/reduce_scatter | solution.py:177
  859.1 32.6 all-gather.3
  936.8 33.7 all-gather.34.cloned.1.call-done
  984.9 313.9 %reduce-scatter.21.cloned.1.call-done = f32[2048,1,576]{0,2,1:T(8,128)} async-done(((f32[2048,4,576]{0,2,1:T(8,128)}), f32[2048,1,576]{0,2,1:T(8,128)}) %reduce-scatter.21.cloned.1.call-update) | async-done | bytes 4718608 | tf_op jit(solution)/shard_map/reduce_scatter | solution.py:177
  1302.6 53.5 %all-gather.44.cloned.1.call-done = bf16[2048,1792]{0,1:T(8,128)(2,1)} async-done(((bf16[2048,448]{0,1:T(8,128)(2,1)}), bf16[2048,1792]{0,1:T(8,128)(2,1)}) %all-gather.44.cloned.1.call-update) | async-done | bytes 7340048 | tf_op jit(solution)/shard_map/all_gather | solution.py:169
  1368.4 74.2 %reduce-scatter.23.cloned.1.call-done = f32[2048,1,128]{0,2,1:T(8,128)} async-done(((f32[2048,4,128]{0,2,1:T(8,128)}), f32[2048,1,128]{0,2,1:T(8,128)}) %reduce-scatter.23.cloned.1.call-update) | async-done | bytes 1048592 | tf_op jit(solution)/shard_map/reduce_scatter | solution.py:177
  1445.7 32.6 all-gather.6
  1520.6 58.6 %all-gather.36.cloned.1.call-done = bf16[4,2048,512]{2,1,0:T(8,128)(2,1)} async-done(((bf16[4,2048,128]{2,1,0:T(8,128)(2,1)}), bf16[4,2048,512]{2,1,0:T(8,128)(2,1)}) %all-gather.36.cloned.1.call-update) | async-done | bytes 8388624 | tf_op jit(solution)/shard_map/all_gather | solution.py:169
  1594.9 279.7 %reduce-scatter.25.cloned.1.call-done = f32[2048,1,512]{0,2,1:T(8,128)} async-done(((f32[2048,4,512]{0,2,1:T(8,128)}), f32[2048,1,512]{0,2,1:T(8,128)}) %reduce-scatter.25.cloned.1.call-update) | async-done | bytes 4194320 | tf_op jit(solution)/shard_map/reduce_scatter | solution.py:177
  1898.2 355.7 %while.73 = (s32[]{:T(128)}, f32[2,64,64]{2,1,0:T(8,128)S(1)}, f32[32,64,2,64]{3,1,2,0:T(8,128)}, f32[2,64]{1,0:T(2,128)S(1)}, f32[32,64]{1,0:T(8,128)}, /*index...) while((s32[]{:T(128)}, f32[2,64,64]{2,1,0:T(8,128)S(1)}, ...), condition=%wide.region_26.27_spmd.clone, body=%wide.region_23.26_spmd.clone.sunk | while | flops 25355200 | bytes 975315 | solution.py:120
  2255.6 331.4 %while.75 = (s32[]{:T(128)}, f32[2,64,64]{2,1,0:T(8,128)S(1)}, f32[32,64,2,64]{3,1,2,0:T(8,128)}, f32[32,2,64,64]{3,2,1,0:T(8,128)}, f32[2,64,1]{1,0,2:T(2,128)S...) while((s32[]{:T(128)}, f32[2,64,64]{2,1,0:T(8,128)S(1)}, ...), condition=%wide.region_46.47_spmd.clone.clone.clone.clone, body=%wide.region_43.46_spmd.clone.clone.clone.clone.sunk | while | flops 25362944 | bytes 1068772 | solution.py:120
  2631.9 76.8 %reduce-scatter.27.cloned.1.call-done = f32[2048,1,128]{0,2,1:T(8,128)} async-done(((f32[2048,4,128]{0,2,1:T(8,128)}), f32[2048,1,128]{0,2,1:T(8,128)}) %reduce-scatter.27.cloned.1.call-update) | async-done | bytes 1048592 | tf_op jit(solution)/shard_map/reduce_scatter | solution.py:177
  2711.1 33.2 all-gather.9
  2787.1 34.1 all-gather.38.cloned.1.call-done
  2835.6 313.9 %reduce-scatter.29.cloned.1.call-done = f32[2048,1,576]{0,2,1:T(8,128)} async-done(((f32[2048,4,576]{0,2,1:T(8,128)}), f32[2048,1,576]{0,2,1:T(8,128)}) %reduce-scatter.29.cloned.1.call-update) | async-done | bytes 4718608 | tf_op jit(solution)/shard_map/reduce_scatter | solution.py:177
  3153.3 53.5 %all-gather.50.cloned.1.call-done = bf16[2048,1792]{0,1:T(8,128)(2,1)} async-done(((bf16[2048,448]{0,1:T(8,128)(2,1)}), bf16[2048,1792]{0,1:T(8,128)(2,1)}) %all-gather.50.cloned.1.call-update) | async-done | bytes 7340048 | tf_op jit(solution)/shard_map/all_gather | solution.py:169
  3216.3 76.9 %reduce-scatter.33.cloned.1.call-done = f32[2048,1,128]{0,2,1:T(8,128)} async-done(((f32[2048,4,128]{0,2,1:T(8,128)}), f32[2048,1,128]{0,2,1:T(8,128)}) %reduce-scatter.33.cloned.1.call-update) | async-done | bytes 1048592 | tf_op jit(solution)/shard_map/reduce_scatter | solution.py:177
  3296.5 46.4 all-gather.48.cloned.1.call-done
  3352.1 64.3 %reduce-scatter.31.cloned.1.call-done = bf16[1,2048,448]{1,2,0:T(8,128)(2,1)} async-done(((bf16[1,2048,1792]{1,2,0:T(8,128)(2,1)}), bf16[1,2048,448]{1,2,0:T(8,128)(2,1)}) %reduce-scatter.31.cloned.1.call-update) | async-done | bytes 1835024 | tf_op jit(solution)/shard_map/reduce_scatter | solution.py:200
  3421.4 166.9 %all-gather.40.cloned.1.call-done = bf16[2048,4,576]{0,2,1:T(8,128)(2,1)} async-done(((bf16[2048,1,576]{0,2,1:T(8,128)(2,1)}), bf16[2048,4,576]{0,2,1:T(8,128)(2,1)}) %all-gather.40.cloned.1.call-update) | async-done | bytes 9437200 | tf_op jit(solution)/shard_map/all_gather | solution.py:182
  3617.4 42.7 reduce-scatter.37.cloned.1.call-done
  3678.2 33.7 all-gather.17
  3714.9 43.8 all-gather.52.cloned.1.call-done
  3815.8 629.8 %while.74 = (s32[]{:T(128)}, f32[2,64]{1,0:T(2,128)S(1)}, f32[2,64]{1,0:T(2,128)S(1)}, f32[2,64,64]{2,1,0:T(8,128)S(1)}, f32[32,64,2,64]{1,0,3,2:T(8,128)}, /*in...) while((s32[]{:T(128)}, f32[2,64]{1,0:T(2,128)S(1)}, ...), condition=%wide.region_62.63_spmd.clone, body=%wide.region_53.62_spmd.clone.sunk | while | flops 57132356 | bytes 2100241 | solution.py:120
  4481.5 126.2 %all-gather.54.cloned.1.call-done = bf16[2048,2048]{0,1:T(8,128)(2,1)} async-done(((bf16[2048,512]{0,1:T(8,128)(2,1)}), bf16[2048,2048]{0,1:T(8,128)(2,1)}) %all-gather.54.cloned.1.call-update) | async-done | bytes 8388624 | tf_op jit(solution)/shard_map/all_gather | solution.py:182
  4670.1 119.0 %all-reduce.17.cloned.1.call-done = (bf16[4,128,512]{2,1,0:T(8,128)(2,1)}, bf16[4,128,512]{2,1,0:T(8,128)(2,1)}, bf16[4,128,512]{2,1,0:T(8,128)(2,1)}, bf16[4,12...) async-done(((bf16[4,128,512]{2,1,0:T(8,128)(2,1)}, ...) | async-done | bytes 6815760 | tf_op jit(solution)/shard_map/psum | solution.py:342
  4802.8 60.6 %reduce-scatter.39.cloned.1.call-done = bf16[128,8192]{1,0:T(8,128)(2,1)} async-done(((bf16[512,8192]{1,0:T(8,128)(2,1)}), bf16[128,8192]{1,0:T(8,128)(2,1)}) %reduce-scatter.39.cloned.1.call-update) | async-done | bytes 2097168
  4885.3 33.8 all-gather.18
  (3710 shorter events, 2254.2 us)
Async XLA Ops:
  7.2 966.4 %copy-start = (bf16[4,448,512]{2,1,0:T(8,128)(2,1)S(1)}, bf16[4,448,512]{2,1,0:T(8,128)(2,1)}, u32[]{:S(2)}) copy-start(bf16[4,448,512]{2,1,0:T(8,128)(2,1)} %param.28) | copy-start | bytes 5505028
  7.2 138.7 %all-gather.32.cloned.1.call-start = ((), (), s32[]{:S(2)}) async-start(), calls=%async_computation.12 | async-start | bytes 10485760 | tf_op jit(solution)/shard_map/all_gather | solution.py:169
  8.1 773.9 %copy-start.40 = (f32[14,128]{1,0:T(8,128)}, f32[14,128]{1,0:T(8,128)S(1)}, u32[]{:S(2)}) copy-start(f32[14,128]{1,0:T(8,128)S(1)} %convert_element_type.306) | copy-start | bytes 21508
  9.2 740.5 %copy-start.52 = (f32[128]{0:T(128)}, f32[128]{0:T(128)S(1)}, u32[]{:S(2)}) copy-start(f32[128]{0:T(128)S(1)} %get-tuple-element.1417) | copy-start | bytes 1540
  9.2 740.5 %copy-start.54 = (f32[128]{0:T(128)}, f32[128]{0:T(128)S(1)}, u32[]{:S(2)}) copy-start(f32[128]{0:T(128)S(1)} %get-tuple-element.1418) | copy-start | bytes 1540
  9.2 1507.9 %copy-start.34 = (f32[4,128]{1,0:T(4,128)}, f32[4,128]{1,0:T(4,128)S(1)}, u32[]{:S(2)}) copy-start(f32[4,128]{1,0:T(4,128)S(1)} %broadcast_subtract_fusion.4) | copy-start | bytes 6148
  87.5 353.8 %reduce-scatter.17.cloned.1.call-start = ((), (), s32[]{:S(2)}) async-start(), calls=%async_computation.13 | async-start | bytes 20971520 | tf_op jit(solution)/shard_map/reduce_scatter | solution.py:177
  160.8 615.0 %all-gather.42.cloned.1.call-start = ((), (), s32[]{:S(2)}) async-start(), calls=%async_computation.27 | async-start | bytes 2621440 | tf_op jit(solution)/shard_map/all_gather | solution.py:169
  161.8 283.1 %copy-start.59 = (f32[2,64]{1,0:T(2,128)}, f32[2,64]{1,0:T(2,128)S(1)}, u32[]{:S(2)}) copy-start(f32[2,64]{1,0:T(2,128)S(1)} %exp.150) | copy-start | bytes 1540
  752.4 105.3 %reduce-scatter.19.cloned.1.call-start = ((), (), s32[]{:S(2)}) async-start(), calls=%async_computation.14 | async-start | bytes 5242880 | tf_op jit(solution)/shard_map/reduce_scatter | solution.py:177
  780.7 189.8 %all-gather.34.cloned.1.call-start = ((), (), s32[]{:S(2)}) async-start(), calls=%async_computation.15 | async-start | bytes 5242880 | tf_op jit(solution)/shard_map/all_gather | solution.py:169
  936.3 362.5 %reduce-scatter.21.cloned.1.call-start = ((), (), s32[]{:S(2)}) async-start(), calls=%async_computation.16 | async-start | bytes 23592960 | tf_op jit(solution)/shard_map/reduce_scatter | solution.py:177
  984.9 371.2 %all-gather.44.cloned.1.call-start = ((), (), s32[]{:S(2)}) async-start(), calls=%async_computation.28 | async-start | bytes 9175040 | tf_op jit(solution)/shard_map/all_gather | solution.py:169
  1302.6 140.1 %reduce-scatter.23.cloned.1.call-start = ((), (), s32[]{:S(2)}) async-start(), calls=%async_computation.17 | async-start | bytes 5242880 | tf_op jit(solution)/shard_map/reduce_scatter | solution.py:177
  1365.8 213.4 %all-gather.36.cloned.1.call-start = ((), (), s32[]{:S(2)}) async-start(), calls=%async_computation.18 | async-start | bytes 10485760 | tf_op jit(solution)/shard_map/all_gather | solution.py:169
  1365.9 1342.8 %copy-start.2 = (f32[2048,128]{0,1:T(8,128)}, f32[2048,128]{0,1:T(8,128)S(1)}, u32[]{:S(2)}) copy-start(f32[2048,128]{0,1:T(8,128)S(1)} %convert_bitcast_fusion) | copy-start | bytes 3145732
  1520.5 354.1 %reduce-scatter.25.cloned.1.call-start = ((), (), s32[]{:S(2)}) async-start(), calls=%async_computation.19 | async-start | bytes 20971520 | tf_op jit(solution)/shard_map/reduce_scatter | solution.py:177
  1594.1 1032.7 %all-gather.46.cloned.1.call-start = ((), (), s32[]{:S(2)}) async-start(), calls=%async_computation.29 | async-start | bytes 2621440 | tf_op jit(solution)/shard_map/all_gather | solution.py:169
  2603.4 105.3 %reduce-scatter.27.cloned.1.call-start = ((), (), s32[]{:S(2)}) async-start(), calls=%async_computation.20 | async-start | bytes 5242880 | tf_op jit(solution)/shard_map/reduce_scatter | solution.py:177
  2631.8 189.4 %all-gather.38.cloned.1.call-start = ((), (), s32[]{:S(2)}) async-start(), calls=%async_computation.21 | async-start | bytes 5242880 | tf_op jit(solution)/shard_map/all_gather | solution.py:169
  2787.1 362.4 %reduce-scatter.29.cloned.1.call-start = ((), (), s32[]{:S(2)}) async-start(), calls=%async_computation.22 | async-start | bytes 23592960 | tf_op jit(solution)/shard_map/reduce_scatter | solution.py:177
  2835.5 371.2 %all-gather.50.cloned.1.call-start = ((), (), s32[]{:S(2)}) async-start(), calls=%async_computation.31 | async-start | bytes 9175040 | tf_op jit(solution)/shard_map/all_gather | solution.py:169
  3153.2 140.0 %reduce-scatter.33.cloned.1.call-start = ((), (), s32[]{:S(2)}) async-start(), calls=%async_computation.24 | async-start | bytes 5242880 | tf_op jit(solution)/shard_map/reduce_scatter | solution.py:177
  3216.3 126.7 %all-gather.48.cloned.1.call-start = ((), (), s32[]{:S(2)}) async-start(), calls=%async_computation.30 | async-start | bytes 2621440 | tf_op jit(solution)/shard_map/all_gather | solution.py:182
  3296.3 120.1 %reduce-scatter.31.cloned.1.call-start = ((), (), s32[]{:S(2)}) async-start(), calls=%async_computation.23 | async-start | bytes 9175040 | tf_op jit(solution)/shard_map/reduce_scatter | solution.py:200
  3352.1 236.3 %all-gather.40.cloned.1.call-start = ((), (), s32[]{:S(2)}) async-start(), calls=%async_computation.25 | async-start | bytes 11796480 | tf_op jit(solution)/shard_map/all_gather | solution.py:182
  3421.4 238.8 %reduce-scatter.37.cloned.1.call-start = ((), (), s32[]{:S(2)}) async-start(), calls=%async_computation.34 | async-start | bytes 5242880
  3617.3 141.4 %all-gather.52.cloned.1.call-start = ((), (), s32[]{:S(2)}) async-start(), calls=%async_computation.32 | async-start | bytes 2621440 | tf_op jit(solution)/shard_map/all_gather | solution.py:182
  3714.9 78.4 %reduce-scatter.35.cloned.1.call-start = ((), (), s32[]{:S(2)}) async-start(), calls=%async_computation.26 | async-start | bytes 2621440 | tf_op jit(solution)/shard_map/reduce_scatter | solution.py:200
  3763.0 844.7 %all-gather.54.cloned.1.call-start = ((), (), s32[]{:S(2)}) async-start(), calls=%async_computation.33 | async-start | bytes 10485760 | tf_op jit(solution)/shard_map/all_gather | solution.py:182
  4457.8 331.3 %all-reduce.17.cloned.1.call-start = ((), (), s32[]{:S(2)}) async-start(), calls=%async_computation.36 | async-start | bytes 13631488 | tf_op jit(solution)/shard_map/psum | solution.py:342
  4623.8 239.7 %reduce-scatter.39.cloned.1.call-start = ((), (), s32[]{:S(2)}) async-start(), calls=%async_computation.35 | async-start | bytes 10485760
  (85 other events, 1632.2 us)
Sparse Core Ops, SparseCore 0:
  87.6 58.2 all-gather.31
  160.9 280.2 reduce-scatter.16
  752.5 23.2 all-gather.41
  780.8 76.7 reduce-scatter.18
  936.5 33.9 all-gather.33
  985.0 313.7 reduce-scatter.20
  1302.7 53.3 all-gather.43
  1365.9 76.7 reduce-scatter.22
  1520.7 58.4 all-gather.35
  1594.2 280.2 reduce-scatter.24
  2603.5 23.3 all-gather.45
  2631.9 76.7 reduce-scatter.26
  2787.2 33.9 all-gather.37
  2835.7 313.7 reduce-scatter.28
  3153.3 53.3 all-gather.49
  3216.4 76.7 reduce-scatter.32
  3296.4 46.4 all-gather.47
  3352.2 64.1 reduce-scatter.30
  3421.5 166.7 all-gather.39
  3617.4 42.6 reduce-scatter.36
  3715.0 43.6 all-gather.51
  3763.1 30.1 reduce-scatter.34
  4458.0 149.6 all-gather.53
  4623.9 165.1 all-reduce.16
  4791.7 71.7 reduce-scatter.38
